TPU v7x, 32 devices: a whole 2x2x4 slice. The times are simulated.
32 devices in a mesh: inner: 4 (over y, x), outer: 8 (over z, core).
Axes of the slice: x: 2, y: 2, z: 4, core: 2. Of those that a mesh axis runs over, the one named last changes fastest.
Arguments:
- jac: float32 [512, 256, 256], P(('outer', 'inner')), may hold values from -0.5 to 1
- obs: float32 [512, 256], P(('outer', 'inner')), may hold values from -6 to 6
- gain_filter: float32 [256], replicated, may hold values from 0 to 0.1
- gain_smooth: float32 [256, 256], replicated, may hold values from -0.5 to 1
- init_mean: float32 [256], replicated, may hold values from -6 to 6
Outputs:
- filtered: float32 [512, 256], P(('outer', 'inner'))
- smoothed: float32 [512, 256], P(('outer', 'inner'))
All inputs are finite; a program needn't handle non-finite values.
Results may differ from a plain program's by a relative error of at most 0.0003.
Values sent between devices are 32-bit elements; how exact they have to be, the bound alone decides.
A program may use at most 64 MiB of HBM per device.

v0:
```python
import jax
import jax.numpy as jnp
from jax import lax
from jax.sharding import PartitionSpec as P

HIGHEST = lax.Precision.HIGHEST


def entering(part, axis, combine, identity):
    place = lax.axis_index(axis)
    gathered = lax.all_gather(part, axis)
    state = jnp.zeros_like(part) + jnp.asarray(identity, part.dtype)

    def one(turn, state):
        return combine(state, lax.dynamic_index_in_dim(gathered, turn, 0, False))

    return lax.fori_loop(0, place, one, state)


def last_row(state_width):
    return (jnp.arange(state_width + 1) == state_width).astype(jnp.float32)[:, None]


def identity_map(state_width):
    return jnp.concatenate(
        [jnp.eye(state_width, dtype=jnp.float32), jnp.zeros((1, state_width), jnp.float32)], 0
    )


def compose(earlier, later):
    state_width = later.shape[1]
    product = jnp.dot(earlier, later[:state_width], precision=HIGHEST)
    return product + last_row(state_width) * later[state_width][None, :]


def advance(packed, state):
    state_width = packed.shape[1]
    return jnp.dot(state, packed[:state_width], precision=HIGHEST) + packed[state_width]


def raise_power(factor, count):
    result = jnp.eye(factor.shape[0], dtype=jnp.float32)
    square = factor
    while count > 0:
        if count % 2 == 1:
            result = jnp.dot(result, square, precision=HIGHEST)
        count = count // 2
        if count > 0:
            square = jnp.dot(square, square, precision=HIGHEST)
    return result


def incoming_state(own_map, boundary):
    state_width = own_map.shape[1]
    identity = identity_map(state_width)
    inner_count = lax.axis_size("inner")
    inner_here = lax.axis_index("inner")
    gathered = lax.all_gather(own_map[None], "inner", axis=0, tiled=True)

    def absorb(running, inputs):
        before, group_total = running
        segment, position = inputs
        group_total = compose(group_total, segment)
        taken = position < inner_here
        before = jnp.where(taken, group_total, before)
        return ((before, group_total), None)

    (seg_before, group_total), _ = lax.scan(
        absorb,
        (identity, identity),
        (gathered, jnp.arange(inner_count, dtype=jnp.int32)),
        reverse=False,
    )
    group_before = entering(group_total, "outer", compose, identity)
    group_state = advance(group_before, boundary)
    return advance(seg_before, group_state)


def entering_backward(offset_sum, step_power):
    inner_count = lax.axis_size("inner")
    inner_here = lax.axis_index("inner")
    outer_count = lax.axis_size("outer")
    outer_here = lax.axis_index("outer")
    zero_state = jnp.zeros_like(offset_sum)
    seg_offsets = lax.all_gather(offset_sum[None], "inner", axis=0, tiled=True)

    def run_affine(power, here):

        def turn(running, inputs):
            state, caught = running
            offset, position = inputs
            caught = jnp.where(position == here, state, caught)
            state = jnp.dot(state, power, precision=HIGHEST) + offset
            return ((state, caught), None)

        return turn

    (group_offset, _), _ = lax.scan(
        run_affine(step_power, inner_here),
        (zero_state, zero_state),
        (seg_offsets, jnp.arange(inner_count, dtype=jnp.int32)),
        reverse=True,
    )
    group_power = raise_power(step_power, inner_count)
    group_offsets = lax.all_gather(group_offset[None], "outer", axis=0, tiled=True)
    (_, group_state), _ = lax.scan(
        run_affine(group_power, outer_here),
        (zero_state, zero_state),
        (group_offsets, jnp.arange(outer_count, dtype=jnp.int32)),
        reverse=True,
    )
    (_, device_state), _ = lax.scan(
        run_affine(step_power, inner_here),
        (group_state, group_state),
        (seg_offsets, jnp.arange(inner_count, dtype=jnp.int32)),
        reverse=True,
    )
    return device_state


def shards(jac, obs, gain_filter, gain_smooth, init_mean):
    state_width = jac.shape[1]
    step_count = jac.shape[0]
    retain = 1.0 - gain_filter
    bottom = last_row(state_width)

    def compose_forward(packed, inputs):
        step_matrix, measured = inputs
        moved = (
            lax.dot_general(packed, step_matrix, (((1,), (1,)), ((), ())), precision=HIGHEST)
            * retain[None, :]
        )
        return (moved + bottom * (gain_filter * measured)[None, :], None)

    forward_map, _ = lax.scan(compose_forward, identity_map(state_width), (jac, obs))
    start_state = incoming_state(forward_map, init_mean)

    def forward(state, inputs):
        step_matrix, measured = inputs
        predicted = jnp.dot(step_matrix, state, precision=HIGHEST)
        updated = predicted + gain_filter * (measured - predicted)
        return (updated, (predicted, updated))

    _, (predicted_all, filtered_all) = lax.scan(forward, start_state, (jac, obs))
    correction = filtered_all - predicted_all

    def backward(state, term):
        renewed = jnp.dot(gain_smooth, state, precision=HIGHEST) + term
        return (renewed, renewed)

    zero_state = jnp.zeros((state_width,), jnp.float32)
    offset_sum, _ = lax.scan(backward, zero_state, correction, reverse=True)
    step_power = raise_power(gain_smooth.T, step_count)
    after_state = entering_backward(offset_sum, step_power)
    _, back_states = lax.scan(backward, after_state, correction, reverse=True)
    return (filtered_all, predicted_all + back_states)


def solution(mesh):
    return jax.shard_map(
        shards,
        mesh=mesh,
        in_specs=(P(("outer", "inner"), None, None), P(("outer", "inner"), None), P(), P(), P()),
        out_specs=(P(("outer", "inner"), None), P(("outer", "inner"), None)),
        check_vma=False,
    )
```

profile of v0, /device:TPU:0, one launch (start us, length us, event | category | flops | bytes accessed | tf_op | source)
XLA Modules:
  0.0 221.8 jit_solution(6826046817942252627)
XLA Ops:
  8.0 34.7 %while.131 = (s32[]{:T(128)}, f32[257,256]{1,0:T(8,128)S(1)}, f32[16,256,256]{2,1,0:T(8,128)}, f32[256]{0:T(256)S(1)}, f32[256]{0:T(256)}, /*index=5*/f32[16,256]{1,0:T(8,128)}, s32[]{:T(128)}) while((s32[]{:T(128)}, f32[257,256]{1,0:T(8,128)S(1)}, f32[16,256,256]{2,1,0:T(8,128)}, f32[256]{0:T(256)S(1)}, f32[256]{0:T(256)}, ...), condition=%wide.region_1.2_spmd.clone, body=%wide.region_0.1_spmd.clone.sunk | while | flops 202311168 | bytes 1322585 | solution.py:135
  8.8 1.4 fusion.109
  10.9 1.4 fusion.109
  15.3 1.4 fusion.109
  19.6 1.4 fusion.109
  23.9 1.4 fusion.109
  28.3 1.4 fusion.109
  32.6 1.4 fusion.109
  37.0 1.4 fusion.109
  41.3 1.4 fusion.109
  43.5 29.5 %all-gather.11.cloned.1.call-done = f32[4,257,256]{2,1,0:T(8,128)} async-done(((f32[1,257,256]{2,1,0:T(8,128)}), f32[4,257,256]{2,1,0:T(8,128)}) %all-gather.11.cloned.1.call-update) | async-done | bytes 1052688 | tf_op jit(solution)/shard_map/all_gather | solution.py:58
  73.1 14.0 %while.126 = (s32[]{:T(128)}, f32[257,256]{1,0:T(8,128)S(1)}, f32[257,256]{1,0:T(8,128)S(1)}, s32[4]{0:T(128)S(1)}, s32[]{:T(128)}, /*index=5*/f32[4,257,256]{2,1,0:T(8,128)}, s32[]{:T(128)}, s32[]{:T(128)}, s32[]{}) while((s32[]{:T(128)}, f32[257,256]{1,0:T(8,128)S(1)}, f32[257,256]{1,0:T(8,128)S(1)}, s32[4]{0:T(128)S(1)}, s32[]{:T(128)}, ...), condition=%wide.region_3.4_spmd, body=%wide.region_2.3_spmd.sunk | while | flops 202310912 | bytes 1846927 | solution.py:68
  75.1 1.5 broadcast_select_fusion.9
  78.6 1.5 broadcast_select_fusion.9
  82.1 1.5 broadcast_select_fusion.9
  85.6 1.5 broadcast_select_fusion.9
  91.0 26.7 %all-gather.13.cloned.1.call-done = f32[8,257,256]{2,1,0:T(8,128)} async-done(((f32[1,257,256]{2,1,0:T(8,128)}), f32[8,257,256]{2,1,0:T(8,128)}) %all-gather.13.cloned.1.call-update) | async-done | bytes 2105360 | tf_op jit(solution)/shard_map/all_gather | solution.py:11
  118.3 33.3 %while.128 = (s32[]{:T(128)}, f32[256]{0:T(256)S(1)}, f32[16,256]{1,0:T(8,128)S(1)}, f32[16,256]{1,0:T(8,128)S(1)}, f32[16,256,256]{2,1,0:T(8,128)}, /*index=5*/...) while((s32[]{:T(128)}, f32[256]{0:T(256)S(1)}, f32[16,256]{1,0:T(8,128)S(1)}, ...), condition=%wide.region_7.8_spmd, body=%wide.region_6.7_spmd.sunk | while | flops 787202 | bytes 275049 | solution.py:144
  151.6 6.1 %while.132 = (s32[]{:T(128)}, f32[256]{0:T(256)S(1)}, f32[256,256]{1,0:T(8,128)S(1)}, f32[16,256]{1,0:T(8,128)S(1)}, s32[]{:T(128)}, /*index=5*/s32[]{:T(128)}, s32[]{:T(128)}) while((s32[]{:T(128)}, f32[256]{0:T(256)S(1)}, f32[256,256]{1,0:T(8,128)S(1)}, f32[16,256]{1,0:T(8,128)S(1)}, s32[]{:T(128)}, /*index=5*/s32[]{:T(128)}, ...), condition=%wide.region_9.10_spmd.clone, body=%wide.region_8.9_spmd.clone.sunk | while | flops 786948 | bytes 271463 | solution.py:152
  157.7 8.0 %all-gather.6 = f32[4,1,256]{2,1,0:T(1,128)S(1)} all-gather(f32[1,1,256]{2,1,0:T(1,128)S(1)} %bitcast.222), channel_id=4, replica_groups=mesh['inner'=4,'outer'=8] {'inner'}, dimensions={0}, use_global_device_ids=true | all-gather | bytes 5120 | tf_op jit(solution)/shard_map/all_gather | solution.py:85
  166.9 22.8 %all-gather.7 = f32[8,1,256]{2,1,0:T(1,128)S(1)} all-gather(f32[1,1,256]{2,1,0:T(1,128)S(1)} %bitcast.221), channel_id=5, replica_groups=mesh['inner'=4,'outer'=8] {'outer'}, dimensions={0}, use_global_device_ids=true | all-gather | bytes 9216 | tf_op jit(solution)/shard_map/all_gather | solution.py:105
  189.7 12.2 %while.134 = (s32[]{:T(128)}, f32[256]{0:T(256)S(1)}, f32[256]{0:T(256)S(1)}, f32[256,256]{1,0:T(8,128)S(1)}, f32[8,256]{1,0:T(8,128)S(1)}, /*index=5*/s32[8]{0:...) while((s32[]{:T(128)}, f32[256]{0:T(256)S(1)}, f32[256]{0:T(256)S(1)}, ...), condition=%wide.region_13.14_spmd.clone, body=%wide.region_12.13_spmd.clone.sunk | while | flops 787461 | bytes 273557 | solution.py:106
  201.9 6.0 %while.129 = (s32[]{:T(128)}, f32[256]{0:T(256)S(1)}, f32[256]{0:T(256)S(1)}, f32[256,256]{1,0:T(8,128)S(1)}, f32[4,256]{1,0:T(4,128)S(1)}, /*index=5*/s32[4]{0:T(128)S(1)}, s32[]{:T(128)}, s32[]{:T(128)}, s32[]{:T(128)}) while((s32[]{:T(128)}, f32[256]{0:T(256)S(1)}, f32[256]{0:T(256)S(1)}, f32[256,256]{1,0:T(8,128)S(1)}, ...), condition=%wide.region_15.16_spmd, body=%wide.region_14.15_spmd.sunk | while | flops 786948 | bytes 272515 | solution.py:112
  207.9 6.3 %while.130 = (s32[]{:T(128)}, f32[256]{0:T(256)S(1)}, f32[16,256]{1,0:T(8,128)S(1)}, f32[256,256]{1,0:T(8,128)S(1)}, f32[16,256]{1,0:T(8,128)S(1)}, /*index=5*/s32[]{:T(128)}, s32[]{:T(128)}, s32[]{:T(128)}) while((s32[]{:T(128)}, f32[256]{0:T(256)S(1)}, f32[16,256]{1,0:T(8,128)S(1)}, f32[256,256]{1,0:T(8,128)S(1)}, ...), condition=%wide.region_17.18_spmd, body=%wide.region_16.17_spmd.sunk | while | flops 786691 | bytes 271465 | solution.py:155
  (408 shorter events, 90.1 us)
Async XLA Ops:
  7.2 110.5 %copy-start = (f32[256]{0:T(256)S(1)}, f32[256]{0:T(256)}, u32[]{:S(2)}) copy-start(f32[256]{0:T(256)} %param.27) | copy-start | bytes 3076
  7.2 65.9 %all-gather.11.cloned.1.call-start = ((), (), s32[]{:S(2)}) async-start(), calls=%async_computation | async-start | bytes 1351680 | tf_op jit(solution)/shard_map/all_gather | solution.py:58
  42.7 0.7 copy-start.3
  43.4 74.2 %all-gather.13.cloned.1.call-start = ((), (), s32[]{:S(2)}) async-start(), calls=%async_computation.1 | async-start | bytes 2433024 | tf_op jit(solution)/shard_map/all_gather | solution.py:11
  73.1 14.8 %copy-start.1 = (f32[256,256]{1,0:T(8,128)S(1)}, f32[256,256]{1,0:T(8,128)}, u32[]{:S(2)}) copy-start(f32[256,256]{1,0:T(8,128)} %param.26) | copy-start | bytes 786436
  87.1 0.7 copy-start.2
  117.6 0.7 copy-start.4
  151.6 38.1 %copy-start.5 = (f32[16,256]{1,0:T(8,128)}, f32[16,256]{1,0:T(8,128)S(1)}, u32[]{:S(2)}) copy-start(f32[16,256]{1,0:T(8,128)S(1)} %get-tuple-element.684) | copy-start | bytes 49156
Sparse Core Ops, SparseCore 0:
  43.5 29.4 all-gather.10
  87.9 29.6 all-gather.12
where the time goes:
time: 225 us; the launch traced here: 222 us
  matrix products  62.5 us (28%)
  waiting for transfers between devices  56.2 us (25%)
  blocking collectives  30.9 us (14%)
  local copies, waits for them, and re-layouts  30.6 us (14%)
  between operations  14.4 us (6%)
  other arithmetic  14.1 us (6%)
  loops' own time  13 us (6%)
    all_gather x1, waiting for transfers between devices, incoming_state(): gathered = lax.all_gather(own_map[None], 'inner', axis=0, tiled=True)  29.5 us
    all_gather x1, waiting for transfers between devices, entering(): gathered = lax.all_gather(part, axis)  26.7 us
    all_gather x1, blocking collectives, entering_backward(): lax.all_gather(group_offset[None], 'outer', axis=0, tiled=True)  22.8 us
    dot_general x16, matrix products, compose_forward(): lax.dot_general(packed, step_matrix, (((1,), (1,)), ((), ())), precision=...  21.9 us
    dot_general x16, matrix products, forward(): predicted = jnp.dot(step_matrix, state, precision=HIGHEST)  19.5 us
    dynamic_slice x48, local copies, waits for them, and re-layouts, shards(): lax.scan(compose_forward, identity_map(state_width), (jac, obs))  13.3 us
    mul x16, other arithmetic, compose_forward(): return (moved + bottom * (gain_filter * measured)[None, :], None)  11.6 us
    dot_general x32, matrix products, backward(): renewed = jnp.dot(gain_smooth, state, precision=HIGHEST) + term  8.65 us
  transfers between devices with their start and end apart: 2, of which 2 were waited for; matrix products, arithmetic and copies ran while one was open for 1% of the time, Pallas kernels for 0%

commit v1 on v0

v1 whole, which is shorter than its diff:
```python
import functools

import jax
import jax.numpy as jnp
from jax import lax
from jax.experimental import pallas as pl
from jax.experimental.pallas import tpu as pltpu
from jax.sharding import PartitionSpec as P

F32 = jnp.float32
BF16 = jnp.bfloat16
MESH = pl.DeviceIdType.MESH


def log2(count):
    assert count & (count - 1) == 0
    return count.bit_length() - 1


def split(x):
    high = x.astype(BF16)
    return high, (x - high.astype(F32)).astype(BF16)


def matmul(a, b):
    dot = functools.partial(jnp.dot, preferred_element_type=F32)
    return dot(a[0], b[0]) + (dot(a[0], b[1]) + dot(a[1], b[0]))


def rows_dot(x, matrix):
    rows = x.shape[0]
    high = x.astype(BF16).astype(F32)
    both = jnp.concatenate([high, x - high], 0).astype(BF16)
    dims = (((1,), (1,)), ((), ()))
    out = lax.dot_general(both, matrix[0], dims, preferred_element_type=F32)
    out = out + lax.dot_general(both, matrix[1], dims, preferred_element_type=F32)
    return out[:rows] + out[rows:]


def kernel(
    inner, outer, block,
    jac_ref, obs_ref, gain_ref, smooth_ref, init_ref,
    filtered_ref, smoothed_ref,
    node_hi, node_lo, power_hi, power_lo, left_hi, left_lo, whole_hi, whole_lo,
    mat_out, mat_in, vec_out, vec_in, down_out, down_in, chain_out, chain_in,
    state_ref, pred_ref, own_ref, gather_ref,
    mat_send, mat_recv, vec_send, vec_recv, down_send, down_recv,
    chain_send, chain_recv, gather_send, gather_recv,
):
    steps, width = obs_ref.shape
    devices = inner * outer
    levels = log2(block)
    me = lax.axis_index("outer") * inner + lax.axis_index("inner")

    def place(device):
        return {"outer": device // inner, "inner": lax.rem(device, inner)}

    def remote(src, dst, send, recv, device):
        return pltpu.make_async_remote_copy(
            src_ref=src, dst_ref=dst, send_sem=send, recv_sem=recv,
            device_id=place(device), device_id_type=MESH,
        )

    gather_ref[...] = jnp.zeros_like(gather_ref)
    barrier = pltpu.get_barrier_semaphore()

    def greet(k, _):
        pl.semaphore_signal(
            barrier, inc=1, device_id=place(lax.rem(me + k, devices)), device_id_type=MESH
        )
        return 0

    lax.fori_loop(1, devices, greet, 0)

    def rep(row):
        return jnp.broadcast_to(row, (8, width))

    def node(i):
        return node_hi[i], node_lo[i]

    def put(hi_ref, lo_ref, i, value):
        hi_ref[i], lo_ref[i] = split(value)

    def power(k):
        return power_hi[k], power_lo[k]

    gain = gain_ref[...]
    retain = 1.0 - gain
    shift = obs_ref[...] * (gain / retain)
    for t in range(steps):
        put(node_hi, node_lo, steps + t, jac_ref[t] * retain)
    for i in range(steps - 1, 0, -1):
        product = matmul(node(2 * i + 1), node(2 * i))
        if i > 1:
            put(node_hi, node_lo, i, product)
        else:
            mat_out[0] = product
            put(node_hi, node_lo, 1, product)

    pl.semaphore_wait(barrier, devices - 1)

    def sends(level):
        span = 2 << level
        return lax.rem(me, span) == span // 2 - 1

    def takes(level):
        span = 2 << level
        return lax.rem(me, span) == span - 1

    def mat_copy(level):
        return remote(
            mat_out.at[level], mat_in.at[level], mat_send.at[level], mat_recv.at[level],
            lax.rem(me + (1 << level), devices),
        )

    def vec_copy(level):
        return remote(
            vec_out.at[level], vec_in.at[level], vec_send.at[level], vec_recv.at[level],
            lax.rem(me + (1 << level), devices),
        )

    @pl.when(sends(0))
    def _():
        mat_copy(0).start()

    offset = {steps + t: rep(shift[t : t + 1]) for t in range(steps)}
    for i in range(steps - 1, 0, -1):
        offset[i] = rows_dot(offset[2 * i], node(2 * i + 1)) + offset[2 * i + 1]
    vec_out[0] = offset[1][:1]

    @pl.when(sends(0))
    def _():
        vec_copy(0).start()

    powers = power_hi.shape[0]
    put(power_hi, power_lo, 0, smooth_ref[...])
    for k in range(1, powers):
        put(power_hi, power_lo, k, matmul(power(k - 1), power(k - 1)))

    for level in range(levels):
        @pl.when(takes(level))
        def _():
            mat_copy(level).wait_recv()
            vec_copy(level).wait_recv()
            own = split(mat_out[level])
            put(left_hi, left_lo, level, mat_in[level])
            product = matmul(own, (left_hi[level], left_lo[level]))
            total = rows_dot(rep(vec_in[level]), own) + vec_out[level]
            if level + 1 < levels:
                mat_out[level + 1] = product
            put(whole_hi, whole_lo, 0, product)
            vec_out[level + 1] = total[:1]

        if level + 1 < levels:
            @pl.when(sends(level + 1))
            def _():
                mat_copy(level + 1).start()
                vec_copy(level + 1).start()

    ends = lax.rem(me, block) == block - 1
    chain = remote(
        chain_out, chain_in, chain_send, chain_recv, lax.rem(me + block, devices)
    )

    @pl.when(jnp.logical_and(ends, me < block))
    def _():
        state_ref[...] = init_ref[...] / retain

    @pl.when(jnp.logical_and(ends, me >= block))
    def _():
        chain.wait_recv()
        state_ref[...] = chain_in[...]

    @pl.when(jnp.logical_and(ends, me < devices - block))
    def _():
        after = rows_dot(rep(state_ref[...]), (whole_hi[0], whole_lo[0]))
        chain_out[...] = after[:1] + vec_out[levels]
        chain.start()

    for level in range(levels - 1, -1, -1):
        down = remote(
            down_out.at[level], down_in.at[level], down_send.at[level], down_recv.at[level],
            lax.rem(me + devices - (1 << level), devices),
        )

        @pl.when(takes(level))
        def _():
            down_out[level] = state_ref[...]
            down.start()
            moved = rows_dot(rep(state_ref[...]), (left_hi[level], left_lo[level]))
            state_ref[...] = moved[:1] + vec_in[level]

        @pl.when(sends(level))
        def _():
            down.wait_recv()
            state_ref[...] = down_in[level]

    state = {1: rep(state_ref[...])}
    for i in range(1, steps):
        state[2 * i] = state[i]
        moved = rows_dot(state[i], node(2 * i))
        state[2 * i + 1] = moved + offset[2 * i]
        if 2 * i >= steps:
            t = 2 * i - steps
            pred_ref[t : t + 1] = moved[:1]
            after = rows_dot(state[2 * i + 1], node(2 * i + 1))
            pred_ref[t + 1 : t + 2] = after[:1]

    pred = pred_ref[...]
    filtered = pred + gain * (obs_ref[...] - pred)
    filtered_ref[...] = filtered
    correction = filtered - pred

    def fold(x, first):
        half = x.shape[0] // 2
        while half >= 1:
            step = power(first + log2(half))
            if half >= 8:
                x = x[:half] + rows_dot(x[half:], step)
            else:
                x = x + rows_dot(pltpu.roll(x, 8 - half, 0), step)
            half //= 2
        return x[:1]

    own_ref[...] = fold(correction, 0)

    def gather_copy(k, device):
        return remote(
            own_ref, gather_ref.at[k - 1], gather_send.at[k - 1], gather_recv.at[k - 1], device
        )

    def give(k, _):
        gather_copy(k, me - k).start()
        return 0

    lax.fori_loop(1, me + 1, give, 0)

    def get(k, _):
        gather_copy(k, lax.rem(me + devices - k, devices)).wait_recv()
        return 0

    lax.fori_loop(1, devices - me, get, 0)
    after = fold(gather_ref[:, 0, :], log2(steps))

    row = lax.broadcasted_iota(jnp.int32, (steps, width), 0)
    entering = rows_dot(rep(after), power(0))
    back = correction + jnp.where(row == steps - 1, entering[:1], 0.0)
    reach = 1
    while reach < steps:
        moved = jnp.where(row < steps - reach, pltpu.roll(back, steps - reach, 0), 0.0)
        back = back + rows_dot(moved, power(log2(reach)))
        reach *= 2
    smoothed_ref[...] = pred + back

    def gave(k, _):
        gather_copy(k, me - k).wait_send()
        return 0

    lax.fori_loop(1, me + 1, gave, 0)

    @pl.when(jnp.logical_and(ends, me < devices - block))
    def _():
        chain.wait_send()

    for level in range(levels):
        @pl.when(sends(level))
        def _():
            mat_copy(level).wait_send()
            vec_copy(level).wait_send()

        @pl.when(takes(level))
        def _():
            remote(
                down_out.at[level], down_in.at[level], down_send.at[level], down_recv.at[level],
                lax.rem(me + devices - (1 << level), devices),
            ).wait_send()


def solution(mesh):
    inner, outer = mesh.shape["inner"], mesh.shape["outer"]
    devices = inner * outer
    block = 2 * inner if outer % 2 == 0 else inner
    levels = log2(block)

    def shards(jac, obs, gain_filter, gain_smooth, init_mean):
        steps, width = obs.shape
        powers = log2(steps) + log2(devices)
        square = (width, width)
        vec = (1, width)
        dma = pltpu.SemaphoreType.DMA
        return pl.pallas_call(
            functools.partial(kernel, inner, outer, block),
            out_shape=[jax.ShapeDtypeStruct((steps, width), F32)] * 2,
            in_specs=[pl.BlockSpec(memory_space=pltpu.VMEM)] * 5,
            out_specs=[pl.BlockSpec(memory_space=pltpu.VMEM)] * 2,
            scratch_shapes=[
                pltpu.VMEM((2 * steps, *square), BF16),
                pltpu.VMEM((2 * steps, *square), BF16),
                pltpu.VMEM((powers, *square), BF16),
                pltpu.VMEM((powers, *square), BF16),
                pltpu.VMEM((levels, *square), BF16),
                pltpu.VMEM((levels, *square), BF16),
                pltpu.VMEM((1, *square), BF16),
                pltpu.VMEM((1, *square), BF16),
                pltpu.VMEM((levels, *square), F32),
                pltpu.VMEM((levels, *square), F32),
                pltpu.VMEM((levels + 1, *vec), F32),
                pltpu.VMEM((levels, *vec), F32),
                pltpu.VMEM((levels, *vec), F32),
                pltpu.VMEM((levels, *vec), F32),
                pltpu.VMEM(vec, F32),
                pltpu.VMEM(vec, F32),
                pltpu.VMEM(vec, F32),
                pltpu.VMEM((steps, width), F32),
                pltpu.VMEM(vec, F32),
                pltpu.VMEM((devices, *vec), F32),
                dma((levels,)), dma((levels,)), dma((levels,)), dma((levels,)),
                dma((levels,)), dma((levels,)), dma, dma,
                dma((devices,)), dma((devices,)),
            ],
            compiler_params=pltpu.CompilerParams(
                collective_id=0, has_side_effects=True, vmem_limit_bytes=48 * 2**20
            ),
        )(jac, obs, gain_filter[None], gain_smooth, init_mean[None])

    return jax.shard_map(
        shards,
        mesh=mesh,
        in_specs=(P(("outer", "inner"), None, None), P(("outer", "inner"), None), P(), P(), P()),
        out_specs=(P(("outer", "inner"), None), P(("outer", "inner"), None)),
        check_vma=False,
    )
```

time: 225 us -> 52.4 us (0.23); the launches traced: 222 us -> 52.1 us
  matrix products: 62.5 us -> 0 us
  waiting for transfers between devices: 56.2 us -> 0 us
  Pallas kernels: 0 us -> 45 us
  blocking collectives: 30.9 us -> 0 us
  local copies, waits for them, and re-layouts: 30.6 us -> 6.42 us
  other arithmetic: 14.1 us -> 0 us
  between operations: 14.4 us -> 0.65 us
  loops' own time: 13 us -> 0 us
    dot_general x94 -> x0, matrix products: 62.5 us -> none  [the longest x16 21.9 us: compose_forward(): lax.dot_general(packed, step_matrix, (((1,), (1,)), ((), ())), precision=...]
    all_gather x2 -> x0, waiting for transfers between devices: 56.2 us -> none  [the longest x1 29.5 us: incoming_state(): gathered = lax.all_gather(own_map[None], 'inner', axis=0, tiled=True)]
    pallas_call x0 -> x1, Pallas kernels: none -> 45 us  [shards(): pl.pallas_call(functools.partial(kernel, inner, outer, block), out_shape=...]
    all_gather x2 -> x0, blocking collectives: 30.9 us -> none  [the longest x1 22.8 us: entering_backward(): lax.all_gather(group_offset[None], 'outer', axis=0, tiled=True)]
    dynamic_slice x80 -> x0, local copies, waits for them, and re-layouts: 23.3 us -> none  [the longest x48 13.3 us: shards(): lax.scan(compose_forward, identity_map(state_width), (jac, obs))]
    another operation x9 -> x0, loops' own time: 13 us -> none  [the longest x1 5.52 us: entering_backward(): lax.scan(run_affine(group_power, outer_here), (zero_state, zero_state), (...]
    mul x16 -> x0, other arithmetic: 11.6 us -> none  [compose_forward(): return (moved + bottom * (gain_filter * measured)[None, :], None)]
    unnamed x18 -> x12, local copies, waits for them, and re-layouts: 1.63 us -> 6.42 us
  transfers between devices with their start and end apart: 2 -> 0, of which waited for: 2 -> 0; matrix products, arithmetic and copies ran while one was open for 1% -> 0% of each run, Pallas kernels for 0% -> 0%
where the time goes in v1:
time: 52.4 us; the launch traced here: 52.1 us
  Pallas kernels  45 us (86%)
  local copies, waits for them, and re-layouts  6.42 us (12%)
  between operations  0.65 us (1%)
    pallas_call x1, Pallas kernels, shards(): pl.pallas_call(functools.partial(kernel, inner, outer, block), out_shape=...  45 us
    unnamed x12, local copies, waits for them, and re-layouts  6.42 us

profile of v1, /device:TPU:0, one launch (start us, length us, event | category | flops | bytes accessed | tf_op | source)
XLA Modules:
  0.0 52.1 jit_solution(1428619531310705539)
XLA Ops:
  0.6 0.0 copy-start
  0.6 2.2 %copy-done = f32[16,256,256]{2,1,0:T(8,128)S(1)} copy-done((f32[16,256,256]{2,1,0:T(8,128)S(1)}, f32[16,256,256]{2,1,0:T(8,128)}, u32[]{:S(2)}) %copy-start) | copy-done | bytes 4194328
  2.8 0.0 copy-start.1
  2.8 0.9 %copy-done.1 = f32[256,256]{1,0:T(8,128)S(1)} copy-done((f32[256,256]{1,0:T(8,128)S(1)}, f32[256,256]{1,0:T(8,128)}, u32[]{:S(2)}) %copy-start.1) | copy-done | bytes 262168
  3.8 0.0 copy-start.2
  3.8 0.7 %copy-done.2 = f32[16,256]{1,0:T(8,128)S(1)} copy-done((f32[16,256]{1,0:T(8,128)S(1)}, f32[16,256]{1,0:T(8,128)}, u32[]{:S(2)}) %copy-start.2) | copy-done | bytes 16408
  4.5 0.0 copy-start.3
  4.5 0.7 %copy-done.3 = f32[256]{0:T(256)S(1)} copy-done((f32[256]{0:T(256)S(1)}, f32[256]{0:T(256)}, u32[]{:S(2)}) %copy-start.3) | copy-done | bytes 1048
  5.2 0.0 copy-start.4
  5.2 0.7 %copy-done.4 = f32[256]{0:T(256)S(1)} copy-done((f32[256]{0:T(256)S(1)}, f32[256]{0:T(256)}, u32[]{:S(2)}) %copy-start.4) | copy-done | bytes 1048
  5.8 45.0 %shard_map.68 = (f32[16,256]{1,0:T(8,128)S(1)}, f32[16,256]{1,0:T(8,128)S(1)}) custom-call(f32[16,256,256]{2,1,0:T(8,128)S(1)} %copy-done, f32[16,256]{1,0:T(8,128)S(1)} %copy-done.2, f32[1,256]{1,0:T(1,128)S(1)} %bitcast.2, f32[256,256]{1,0:T(8,128)S(1)} %copy-done.1, f32[1,256]{1,0:T(1,128)S(1)} %bitcast.3), custom_call_target="tpu_custom_call" | custom-call | tf_op jit(solution)/shard_map/pallas_call | solution.py:291
  50.9 0.6 %copy.9 = f32[16,256]{1,0:T(8,128)} copy(f32[16,256]{1,0:T(8,128)S(1)} %get-tuple-element.4) | data formatting | bytes 32768
  51.5 0.6 %copy.10 = f32[16,256]{1,0:T(8,128)} copy(f32[16,256]{1,0:T(8,128)S(1)} %get-tuple-element.5) | data formatting | bytes 32768
Async XLA Ops:
  0.6 2.2 %copy-start = (f32[16,256,256]{2,1,0:T(8,128)S(1)}, f32[16,256,256]{2,1,0:T(8,128)}, u32[]{:S(2)}) copy-start(f32[16,256,256]{2,1,0:T(8,128)} %jac_ref.1) | copy-start | bytes 12582916
  2.8 0.9 %copy-start.1 = (f32[256,256]{1,0:T(8,128)S(1)}, f32[256,256]{1,0:T(8,128)}, u32[]{:S(2)}) copy-start(f32[256,256]{1,0:T(8,128)} %smooth_ref.1) | copy-start | bytes 786436
  3.8 0.7 %copy-start.2 = (f32[16,256]{1,0:T(8,128)S(1)}, f32[16,256]{1,0:T(8,128)}, u32[]{:S(2)}) copy-start(f32[16,256]{1,0:T(8,128)} %obs_ref.1) | copy-start | bytes 49156
  4.5 0.7 %copy-start.3 = (f32[256]{0:T(256)S(1)}, f32[256]{0:T(256)}, u32[]{:S(2)}) copy-start(f32[256]{0:T(256)} %param.7) | copy-start | bytes 3076
  5.2 0.7 %copy-start.4 = (f32[256]{0:T(256)S(1)}, f32[256]{0:T(256)}, u32[]{:S(2)}) copy-start(f32[256]{0:T(256)} %param.9) | copy-start | bytes 3076

commit v2 on v1

--- a/solution.py
+++ b/solution.py
@@ -22,26 +22,41 @@
     return high, (x - high.astype(F32)).astype(BF16)
 
 
-def matmul(a, b):
-    dot = functools.partial(jnp.dot, preferred_element_type=F32)
-    return dot(a[0], b[0]) + (dot(a[0], b[1]) + dot(a[1], b[0]))
-
-
-def rows_dot(x, matrix):
+def split3(x):
+    high = x.astype(BF16)
+    rest = x - high.astype(F32)
+    middle = rest.astype(BF16)
+    return high, middle, (rest - middle.astype(F32)).astype(BF16)
+
+
+def matmul(a, b, turned=False):
+    dims = (((1,), (1 if turned else 0,)), ((), ()))
+
+    def dot(i, j):
+        return lax.dot_general(a[i], b[j], dims, preferred_element_type=F32)
+
+    total = dot(0, 1) + dot(1, 0)
+    if len(a) == 3:
+        total = total + (dot(1, 1) + (dot(0, 2) + dot(2, 0)))
+    return dot(0, 0) + total
+
+
+def rows_dot(x, matrix, turned=True):
     rows = x.shape[0]
     high = x.astype(BF16).astype(F32)
     both = jnp.concatenate([high, x - high], 0).astype(BF16)
-    dims = (((1,), (1,)), ((), ()))
+    dims = (((1,), (1 if turned else 0,)), ((), ()))
     out = lax.dot_general(both, matrix[0], dims, preferred_element_type=F32)
     out = out + lax.dot_general(both, matrix[1], dims, preferred_element_type=F32)
     return out[:rows] + out[rows:]
 
 
 def kernel(
-    inner, outer, block,
+    inner, outer, block, chunks,
     jac_ref, obs_ref, gain_ref, smooth_ref, init_ref,
     filtered_ref, smoothed_ref,
-    node_hi, node_lo, power_hi, power_lo, left_hi, left_lo, whole_hi, whole_lo,
+    node_hi, node_lo, node_end, turned_ref, power_hi, power_lo, power_end,
+    left_hi, left_lo, whole_hi, whole_lo,
     mat_out, mat_in, vec_out, vec_in, down_out, down_in, chain_out, chain_in,
     state_ref, pred_ref, own_ref, gather_ref,
     mat_send, mat_recv, vec_send, vec_recv, down_send, down_recv,
@@ -78,8 +93,11 @@
     def node(i):
         return node_hi[i], node_lo[i]
 
-    def put(hi_ref, lo_ref, i, value):
-        hi_ref[i], lo_ref[i] = split(value)
+    def node3(i):
+        return node_hi[i], node_lo[i], node_end[i]
+
+    def put_node(i, value):
+        node_hi[i], node_lo[i], node_end[i] = split3(value)
 
     def power(k):
         return power_hi[k], power_lo[k]
@@ -88,14 +106,15 @@
     retain = 1.0 - gain
     shift = obs_ref[...] * (gain / retain)
     for t in range(steps):
-        put(node_hi, node_lo, steps + t, jac_ref[t] * retain)
-    for i in range(steps - 1, 0, -1):
-        product = matmul(node(2 * i + 1), node(2 * i))
-        if i > 1:
-            put(node_hi, node_lo, i, product)
-        else:
-            mat_out[0] = product
-            put(node_hi, node_lo, 1, product)
+        put_node(steps + t, jac_ref[t] * retain)
+    for i in range(steps - 1, 1, -1):
+        put_node(i, matmul(node3(2 * i + 1), node3(2 * i)))
+    grid = (width, width)
+    eye = lax.broadcasted_iota(jnp.int32, grid, 0) == lax.broadcasted_iota(jnp.int32, grid, 1)
+    eye = jnp.where(eye, 1.0, 0.0).astype(BF16)
+    for k, piece in enumerate(node3(2)):
+        turned = lax.dot_general(eye, piece, (((1,), (1,)), ((), ())), preferred_element_type=F32)
+        turned_ref[k] = turned.astype(BF16)
 
     pl.semaphore_wait(barrier, devices - 1)
 
@@ -107,9 +126,13 @@
         span = 2 << level
         return lax.rem(me, span) == span - 1
 
-    def mat_copy(level):
+    chunk = width // chunks
+
+    def mat_copy(level, part):
+        rows = pl.ds(part * chunk, chunk)
         return remote(
-            mat_out.at[level], mat_in.at[level], mat_send.at[level], mat_recv.at[level],
+            mat_out.at[level, rows], mat_in.at[level, rows],
+            mat_send.at[level, part], mat_recv.at[level, part],
             lax.rem(me + (1 << level), devices),
         )
 
@@ -119,9 +142,15 @@
             lax.rem(me + (1 << level), devices),
         )
 
-    @pl.when(sends(0))
-    def _():
-        mat_copy(0).start()
+    last = node3(3)
+    for part in range(chunks):
+        rows = slice(part * chunk, (part + 1) * chunk)
+        first = turned_ref[0, rows], turned_ref[1, rows], turned_ref[2, rows]
+        mat_out[0, rows] = matmul(first, last, True)
+
+        @pl.when(sends(0))
+        def _():
+            mat_copy(0, part).start()
 
     offset = {steps + t: rep(shift[t : t + 1]) for t in range(steps)}
     for i in range(steps - 1, 0, -1):
@@ -133,29 +162,40 @@
         vec_copy(0).start()
 
     powers = power_hi.shape[0]
-    put(power_hi, power_lo, 0, smooth_ref[...])
+
+    def put_power(k, value):
+        power_hi[k], power_lo[k], power_end[k] = split3(value)
+
+    put_power(0, smooth_ref[...])
     for k in range(1, powers):
-        put(power_hi, power_lo, k, matmul(power(k - 1), power(k - 1)))
+        base = power_hi[k - 1], power_lo[k - 1], power_end[k - 1]
+        put_power(k, matmul(base, base))
 
     for level in range(levels):
         @pl.when(takes(level))
         def _():
-            mat_copy(level).wait_recv()
+            own = split(mat_out[level])
+            for part in range(chunks):
+                rows = slice(part * chunk, (part + 1) * chunk)
+                mat_copy(level, part).wait_recv()
+                arrived = split(mat_in[level, rows])
+                left_hi[level, rows], left_lo[level, rows] = arrived
+                product = matmul(arrived, own)
+                if level + 1 < levels:
+                    mat_out[level + 1, rows] = product
+
+                    @pl.when(sends(level + 1))
+                    def _():
+                        mat_copy(level + 1, part).start()
+                else:
+                    whole_hi[0, rows], whole_lo[0, rows] = split(product)
             vec_copy(level).wait_recv()
-            own = split(mat_out[level])
-            put(left_hi, left_lo, level, mat_in[level])
-            product = matmul(own, (left_hi[level], left_lo[level]))
-            total = rows_dot(rep(vec_in[level]), own) + vec_out[level]
+            total = rows_dot(rep(vec_in[level]), own, False) + vec_out[level]
+            vec_out[level + 1] = total[:1]
             if level + 1 < levels:
-                mat_out[level + 1] = product
-            put(whole_hi, whole_lo, 0, product)
-            vec_out[level + 1] = total[:1]
-
-        if level + 1 < levels:
-            @pl.when(sends(level + 1))
-            def _():
-                mat_copy(level + 1).start()
-                vec_copy(level + 1).start()
+                @pl.when(sends(level + 1))
+                def _():
+                    vec_copy(level + 1).start()
 
     ends = lax.rem(me, block) == block - 1
     chain = remote(
@@ -173,27 +213,38 @@
 
     @pl.when(jnp.logical_and(ends, me < devices - block))
     def _():
-        after = rows_dot(rep(state_ref[...]), (whole_hi[0], whole_lo[0]))
+        after = rows_dot(rep(state_ref[...]), (whole_hi[0], whole_lo[0]), False)
         chain_out[...] = after[:1] + vec_out[levels]
         chain.start()
 
+    def down(level, reach):
+        return remote(
+            down_out.at[level], down_in,
+            down_send.at[level, reach], down_recv,
+            lax.rem(me + devices + (1 << reach) - (2 << level), devices),
+        )
+
+    def gives(level):
+        if level == levels - 1:
+            return ends
+        return takes(level + 1)
+
+    @pl.when(jnp.logical_not(ends))
+    def _():
+        down(0, 0).wait_recv()
+        state_ref[...] = down_in[...]
+
     for level in range(levels - 1, -1, -1):
-        down = remote(
-            down_out.at[level], down_in.at[level], down_send.at[level], down_recv.at[level],
-            lax.rem(me + devices - (1 << level), devices),
-        )
+        @pl.when(gives(level))
+        def _():
+            down_out[level] = state_ref[...]
+            for reach in range(level, -1, -1):
+                down(level, reach).start()
 
         @pl.when(takes(level))
         def _():
-            down_out[level] = state_ref[...]
-            down.start()
-            moved = rows_dot(rep(state_ref[...]), (left_hi[level], left_lo[level]))
+            moved = rows_dot(rep(state_ref[...]), (left_hi[level], left_lo[level]), False)
             state_ref[...] = moved[:1] + vec_in[level]
-
-        @pl.when(sends(level))
-        def _():
-            down.wait_recv()
-            state_ref[...] = down_in[level]
 
     state = {1: rep(state_ref[...])}
     for i in range(1, steps):
@@ -265,15 +316,14 @@
     for level in range(levels):
         @pl.when(sends(level))
         def _():
-            mat_copy(level).wait_send()
+            for part in range(chunks):
+                mat_copy(level, part).wait_send()
             vec_copy(level).wait_send()
 
-        @pl.when(takes(level))
-        def _():
-            remote(
-                down_out.at[level], down_in.at[level], down_send.at[level], down_recv.at[level],
-                lax.rem(me + devices - (1 << level), devices),
-            ).wait_send()
+        @pl.when(gives(level))
+        def _():
+            for reach in range(level + 1):
+                down(level, reach).wait_send()
 
 
 def solution(mesh):
@@ -281,6 +331,7 @@
     devices = inner * outer
     block = 2 * inner if outer % 2 == 0 else inner
     levels = log2(block)
+    chunks = 4
 
     def shards(jac, obs, gain_filter, gain_smooth, init_mean):
         steps, width = obs.shape
@@ -289,13 +340,16 @@
         vec = (1, width)
         dma = pltpu.SemaphoreType.DMA
         return pl.pallas_call(
-            functools.partial(kernel, inner, outer, block),
+            functools.partial(kernel, inner, outer, block, chunks),
             out_shape=[jax.ShapeDtypeStruct((steps, width), F32)] * 2,
             in_specs=[pl.BlockSpec(memory_space=pltpu.VMEM)] * 5,
             out_specs=[pl.BlockSpec(memory_space=pltpu.VMEM)] * 2,
             scratch_shapes=[
                 pltpu.VMEM((2 * steps, *square), BF16),
                 pltpu.VMEM((2 * steps, *square), BF16),
+                pltpu.VMEM((2 * steps, *square), BF16),
+                pltpu.VMEM((3, *square), BF16),
+                pltpu.VMEM((powers, *square), BF16),
                 pltpu.VMEM((powers, *square), BF16),
                 pltpu.VMEM((powers, *square), BF16),
                 pltpu.VMEM((levels, *square), BF16),
@@ -307,15 +361,15 @@
                 pltpu.VMEM((levels + 1, *vec), F32),
                 pltpu.VMEM((levels, *vec), F32),
                 pltpu.VMEM((levels, *vec), F32),
-                pltpu.VMEM((levels, *vec), F32),
+                pltpu.VMEM(vec, F32),
                 pltpu.VMEM(vec, F32),
                 pltpu.VMEM(vec, F32),
                 pltpu.VMEM(vec, F32),
                 pltpu.VMEM((steps, width), F32),
                 pltpu.VMEM(vec, F32),
                 pltpu.VMEM((devices, *vec), F32),
-                dma((levels,)), dma((levels,)), dma((levels,)), dma((levels,)),
-                dma((levels,)), dma((levels,)), dma, dma,
+                dma((levels, chunks)), dma((levels, chunks)), dma((levels,)), dma((levels,)),
+                dma((levels, levels)), dma, dma, dma,
                 dma((devices,)), dma((devices,)),
             ],
             compiler_params=pltpu.CompilerParams(

time: 52.4 us -> 50.1 us (0.956)
  Pallas kernels: 45 us -> 42.7 us
    pallas_call x1, Pallas kernels: 45 us -> 42.7 us  [shards(): pl.pallas_call(functools.partial(kernel, inner, outer, block, chunks), ou...]
where the time goes in v2:
time: 50.1 us; the launch traced here: 49.8 us
  Pallas kernels  42.7 us (85%)
  local copies, waits for them, and re-layouts  6.42 us (13%)
  between operations  0.65 us (1%)
    pallas_call x1, Pallas kernels, shards(): pl.pallas_call(functools.partial(kernel, inner, outer, block, chunks), ou...  42.7 us
    unnamed x12, local copies, waits for them, and re-layouts  6.42 us

profile of v2, /device:TPU:0, one launch (start us, length us, event | category | flops | bytes accessed | tf_op | source)
XLA Modules:
  0.0 49.8 jit_solution(9175445109245786559)
XLA Ops:
  0.6 0.0 copy-start
  0.6 2.2 %copy-done = f32[16,256,256]{2,1,0:T(8,128)S(1)} copy-done((f32[16,256,256]{2,1,0:T(8,128)S(1)}, f32[16,256,256]{2,1,0:T(8,128)}, u32[]{:S(2)}) %copy-start) | copy-done | bytes 4194328
  2.8 0.0 copy-start.1
  2.8 0.9 %copy-done.1 = f32[256,256]{1,0:T(8,128)S(1)} copy-done((f32[256,256]{1,0:T(8,128)S(1)}, f32[256,256]{1,0:T(8,128)}, u32[]{:S(2)}) %copy-start.1) | copy-done | bytes 262168
  3.8 0.0 copy-start.2
  3.8 0.7 %copy-done.2 = f32[16,256]{1,0:T(8,128)S(1)} copy-done((f32[16,256]{1,0:T(8,128)S(1)}, f32[16,256]{1,0:T(8,128)}, u32[]{:S(2)}) %copy-start.2) | copy-done | bytes 16408
  4.5 0.0 copy-start.3
  4.5 0.7 %copy-done.3 = f32[256]{0:T(256)S(1)} copy-done((f32[256]{0:T(256)S(1)}, f32[256]{0:T(256)}, u32[]{:S(2)}) %copy-start.3) | copy-done | bytes 1048
  5.2 0.0 copy-start.4
  5.2 0.7 %copy-done.4 = f32[256]{0:T(256)S(1)} copy-done((f32[256]{0:T(256)S(1)}, f32[256]{0:T(256)}, u32[]{:S(2)}) %copy-start.4) | copy-done | bytes 1048
  5.8 42.7 %shard_map.68 = (f32[16,256]{1,0:T(8,128)S(1)}, f32[16,256]{1,0:T(8,128)S(1)}) custom-call(f32[16,256,256]{2,1,0:T(8,128)S(1)} %copy-done, f32[16,256]{1,0:T(8,128)S(1)} %copy-done.2, f32[1,256]{1,0:T(1,128)S(1)} %bitcast.2, f32[256,256]{1,0:T(8,128)S(1)} %copy-done.1, f32[1,256]{1,0:T(1,128)S(1)} %bitcast.3), custom_call_target="tpu_custom_call" | custom-call | tf_op jit(solution)/shard_map/pallas_call | solution.py:342
  48.6 0.6 %copy.9 = f32[16,256]{1,0:T(8,128)} copy(f32[16,256]{1,0:T(8,128)S(1)} %get-tuple-element.4) | data formatting | bytes 32768
  49.2 0.6 %copy.10 = f32[16,256]{1,0:T(8,128)} copy(f32[16,256]{1,0:T(8,128)S(1)} %get-tuple-element.5) | data formatting | bytes 32768
Async XLA Ops:
  0.6 2.2 %copy-start = (f32[16,256,256]{2,1,0:T(8,128)S(1)}, f32[16,256,256]{2,1,0:T(8,128)}, u32[]{:S(2)}) copy-start(f32[16,256,256]{2,1,0:T(8,128)} %jac_ref.1) | copy-start | bytes 12582916
  2.8 0.9 %copy-start.1 = (f32[256,256]{1,0:T(8,128)S(1)}, f32[256,256]{1,0:T(8,128)}, u32[]{:S(2)}) copy-start(f32[256,256]{1,0:T(8,128)} %smooth_ref.1) | copy-start | bytes 786436
  3.8 0.7 %copy-start.2 = (f32[16,256]{1,0:T(8,128)S(1)}, f32[16,256]{1,0:T(8,128)}, u32[]{:S(2)}) copy-start(f32[16,256]{1,0:T(8,128)} %obs_ref.1) | copy-start | bytes 49156
  4.5 0.7 %copy-start.3 = (f32[256]{0:T(256)S(1)}, f32[256]{0:T(256)}, u32[]{:S(2)}) copy-start(f32[256]{0:T(256)} %param.7) | copy-start | bytes 3076
  5.2 0.7 %copy-start.4 = (f32[256]{0:T(256)S(1)}, f32[256]{0:T(256)}, u32[]{:S(2)}) copy-start(f32[256]{0:T(256)} %param.9) | copy-start | bytes 3076

commit v3 on v2

--- a/solution.py
+++ b/solution.py
@@ -15,6 +15,22 @@
 def log2(count):
     assert count & (count - 1) == 0
     return count.bit_length() - 1
+
+
+def factors(count):
+    found = []
+    while count > 1:
+        found.append(2)
+        count //= found[-1]
+    return found
+
+
+def exponents_of(steps, devices):
+    found, unit = [], 1
+    for factor in factors(steps) + factors(devices):
+        found += [unit * k for k in range(1, factor)]
+        unit *= factor
+    return found
 
 
 def split(x):
@@ -53,8 +69,9 @@
 
 def kernel(
     inner, outer, block, chunks,
-    jac_ref, obs_ref, gain_ref, smooth_ref, init_ref,
+    jac_hbm, obs_hbm, gain_hbm, smooth_hbm, init_hbm,
     filtered_ref, smoothed_ref,
+    jac_ref, obs_ref, gain_ref, smooth_ref, init_ref, jac_sem, arg_sem,
     node_hi, node_lo, node_end, turned_ref, power_hi, power_lo, power_end,
     left_hi, left_lo, whole_hi, whole_lo,
     mat_out, mat_in, vec_out, vec_in, down_out, down_in, chain_out, chain_in,
@@ -62,13 +79,13 @@
     mat_send, mat_recv, vec_send, vec_recv, down_send, down_recv,
     chain_send, chain_recv, gather_send, gather_recv,
 ):
-    steps, width = obs_ref.shape
+    steps, width = obs_hbm.shape
     devices = inner * outer
     levels = log2(block)
     me = lax.axis_index("outer") * inner + lax.axis_index("inner")
 
     def place(device):
-        return {"outer": device // inner, "inner": lax.rem(device, inner)}
+        return {"outer": lax.div(device, inner), "inner": lax.rem(device, inner)}
 
     def remote(src, dst, send, recv, device):
         return pltpu.make_async_remote_copy(
@@ -76,16 +93,45 @@
             device_id=place(device), device_id_type=MESH,
         )
 
+    sources = (obs_hbm, gain_hbm, smooth_hbm, init_hbm)
+    targets = (obs_ref, gain_ref, smooth_ref, init_ref)
+    arg_copies = [
+        pltpu.make_async_copy(source, target, arg_sem.at[k])
+        for k, (source, target) in enumerate(zip(sources, targets))
+    ]
+    jac_copies = [
+        pltpu.make_async_copy(jac_hbm.at[t], jac_ref.at[t], jac_sem.at[t]) for t in range(steps)
+    ]
+    for copy in arg_copies[:2] + jac_copies + arg_copies[2:]:
+        copy.start()
     gather_ref[...] = jnp.zeros_like(gather_ref)
     barrier = pltpu.get_barrier_semaphore()
 
-    def greet(k, _):
-        pl.semaphore_signal(
-            barrier, inc=1, device_id=place(lax.rem(me + k, devices)), device_id_type=MESH
-        )
-        return 0
-
-    lax.fori_loop(1, devices, greet, 0)
+    def greet(device):
+        pl.semaphore_signal(barrier, inc=1, device_id=place(device), device_id_type=MESH)
+
+    def sends(level):
+        span = 2 << level
+        return lax.rem(me, span) == span // 2 - 1
+
+    def takes(level):
+        span = 2 << level
+        return lax.rem(me, span) == span - 1
+
+    for level in range(levels):
+        @pl.when(takes(level))
+        def _():
+            greet(lax.rem(me + devices - (1 << level), devices))
+
+    ends = lax.rem(me, block) == block - 1
+
+    @pl.when(jnp.logical_and(ends, me >= block))
+    def _():
+        greet(lax.rem(me + devices - block, devices))
+
+    @pl.when(me == devices - 2)
+    def _():
+        greet(lax.rem(me + 1, devices))
 
     def rep(row):
         return jnp.broadcast_to(row, (8, width))
@@ -99,16 +145,34 @@
     def put_node(i, value):
         node_hi[i], node_lo[i], node_end[i] = split3(value)
 
-    def power(k):
+    exponents = exponents_of(steps, devices)
+
+    def power(exponent):
+        k = exponents.index(exponent)
         return power_hi[k], power_lo[k]
 
+    def power3(exponent):
+        k = exponents.index(exponent)
+        return power_hi[k], power_lo[k], power_end[k]
+
+    arg_copies[0].wait()
+    arg_copies[1].wait()
     gain = gain_ref[...]
     retain = 1.0 - gain
     shift = obs_ref[...] * (gain / retain)
-    for t in range(steps):
-        put_node(steps + t, jac_ref[t] * retain)
-    for i in range(steps - 1, 1, -1):
+    group = min(4, steps)
+    for start in range(0, steps, group):
+        for t in range(start, start + group):
+            jac_copies[t].wait()
+        for t in range(start, start + group):
+            put_node(steps + t, jac_ref[t] * retain)
+        for t in range(start, start + group, 2):
+            i = (steps + t) // 2
+            put_node(i, matmul(node3(2 * i + 1), node3(2 * i)))
+    for i in range(steps // 2 - 1, 1, -1):
         put_node(i, matmul(node3(2 * i + 1), node3(2 * i)))
+    for copy in arg_copies[2:]:
+        copy.wait()
     grid = (width, width)
     eye = lax.broadcasted_iota(jnp.int32, grid, 0) == lax.broadcasted_iota(jnp.int32, grid, 1)
     eye = jnp.where(eye, 1.0, 0.0).astype(BF16)
@@ -116,15 +180,7 @@
         turned = lax.dot_general(eye, piece, (((1,), (1,)), ((), ())), preferred_element_type=F32)
         turned_ref[k] = turned.astype(BF16)
 
-    pl.semaphore_wait(barrier, devices - 1)
-
-    def sends(level):
-        span = 2 << level
-        return lax.rem(me, span) == span // 2 - 1
-
-    def takes(level):
-        span = 2 << level
-        return lax.rem(me, span) == span - 1
+    pl.semaphore_wait(barrier, 1)
 
     chunk = width // chunks
 
@@ -161,15 +217,21 @@
     def _():
         vec_copy(0).start()
 
-    powers = power_hi.shape[0]
-
-    def put_power(k, value):
-        power_hi[k], power_lo[k], power_end[k] = split3(value)
-
-    put_power(0, smooth_ref[...])
-    for k in range(1, powers):
-        base = power_hi[k - 1], power_lo[k - 1], power_end[k - 1]
-        put_power(k, matmul(base, base))
+    def raise_powers(some):
+        for exponent in some:
+            k = exponents.index(exponent)
+            if exponent == 1:
+                value = smooth_ref[...]
+            elif exponent % 2:
+                value = matmul(power3(exponent - 1), power3(1))
+            elif exponent // 2 in exponents:
+                value = matmul(power3(exponent // 2), power3(exponent // 2))
+            else:
+                unit = exponents[k - 2]
+                value = matmul(power3(exponents[k - 1]), power3(unit))
+            power_hi[k], power_lo[k], power_end[k] = split3(value)
+
+    raise_powers([e for e in exponents if e < steps])
 
     for level in range(levels):
         @pl.when(takes(level))
@@ -197,7 +259,6 @@
                 def _():
                     vec_copy(level + 1).start()
 
-    ends = lax.rem(me, block) == block - 1
     chain = remote(
         chain_out, chain_in, chain_send, chain_recv, lax.rem(me + block, devices)
     )
@@ -265,7 +326,7 @@
     def fold(x, first):
         half = x.shape[0] // 2
         while half >= 1:
-            step = power(first + log2(half))
+            step = power(first * half)
             if half >= 8:
                 x = x[:half] + rows_dot(x[half:], step)
             else:
@@ -273,33 +334,34 @@
             half //= 2
         return x[:1]
 
-    own_ref[...] = fold(correction, 0)
+    own_ref[...] = fold(correction, 1)
 
     def gather_copy(k, device):
         return remote(
             own_ref, gather_ref.at[k - 1], gather_send.at[k - 1], gather_recv.at[k - 1], device
         )
 
-    def give(k, _):
-        gather_copy(k, me - k).start()
+    def give(device, _):
+        gather_copy(me - device, device).start()
         return 0
 
-    lax.fori_loop(1, me + 1, give, 0)
+    lax.fori_loop(0, me, give, 0)
+    raise_powers([e for e in exponents if e >= steps])
 
     def get(k, _):
         gather_copy(k, lax.rem(me + devices - k, devices)).wait_recv()
         return 0
 
     lax.fori_loop(1, devices - me, get, 0)
-    after = fold(gather_ref[:, 0, :], log2(steps))
+    after = fold(gather_ref[:, 0, :], steps)
 
     row = lax.broadcasted_iota(jnp.int32, (steps, width), 0)
-    entering = rows_dot(rep(after), power(0))
+    entering = rows_dot(rep(after), power(1))
     back = correction + jnp.where(row == steps - 1, entering[:1], 0.0)
     reach = 1
     while reach < steps:
         moved = jnp.where(row < steps - reach, pltpu.roll(back, steps - reach, 0), 0.0)
-        back = back + rows_dot(moved, power(log2(reach)))
+        back = back + rows_dot(moved, power(reach))
         reach *= 2
     smoothed_ref[...] = pred + back
 
@@ -335,16 +397,23 @@
 
     def shards(jac, obs, gain_filter, gain_smooth, init_mean):
         steps, width = obs.shape
-        powers = log2(steps) + log2(devices)
+        powers = len(exponents_of(steps, devices))
         square = (width, width)
         vec = (1, width)
         dma = pltpu.SemaphoreType.DMA
         return pl.pallas_call(
             functools.partial(kernel, inner, outer, block, chunks),
             out_shape=[jax.ShapeDtypeStruct((steps, width), F32)] * 2,
-            in_specs=[pl.BlockSpec(memory_space=pltpu.VMEM)] * 5,
+            in_specs=[pl.BlockSpec(memory_space=pl.ANY)] * 5,
             out_specs=[pl.BlockSpec(memory_space=pltpu.VMEM)] * 2,
             scratch_shapes=[
+                pltpu.VMEM((steps, *square), F32),
+                pltpu.VMEM((steps, width), F32),
+                pltpu.VMEM(vec, F32),
+                pltpu.VMEM(square, F32),
+                pltpu.VMEM(vec, F32),
+                dma((steps,)),
+                dma((4,)),
                 pltpu.VMEM((2 * steps, *square), BF16),
                 pltpu.VMEM((2 * steps, *square), BF16),
                 pltpu.VMEM((2 * steps, *square), BF16),
@@ -373,7 +442,7 @@
                 dma((devices,)), dma((devices,)),
             ],
             compiler_params=pltpu.CompilerParams(
-                collective_id=0, has_side_effects=True, vmem_limit_bytes=48 * 2**20
+                collective_id=0, has_side_effects=True, vmem_limit_bytes=60 * 2**20
             ),
         )(jac, obs, gain_filter[None], gain_smooth, init_mean[None])
 

time: 50.1 us -> 45.7 us (0.912)
  local copies, waits for them, and re-layouts: 6.42 us -> 2.65 us
  Pallas kernels: 42.7 us -> 42 us
    unnamed x12 -> x2, local copies, waits for them, and re-layouts: 6.42 us -> 2.65 us
    pallas_call x1, Pallas kernels: 42.7 us -> 42 us  [shards(): pl.pallas_call(functools.partial(kernel, inner, outer, block, chunks), ou...]
where the time goes in v3:
time: 45.7 us; the launch traced here: 45.3 us
  Pallas kernels  42 us (92%)
  local copies, waits for them, and re-layouts  2.65 us (6%)
  between operations  0.64 us (1%)
    pallas_call x1, Pallas kernels, shards(): pl.pallas_call(functools.partial(kernel, inner, outer, block, chunks), ou...  42 us
    unnamed x2, local copies, waits for them, and re-layouts  2.65 us

profile of v3, /device:TPU:0, one launch (start us, length us, event | category | flops | bytes accessed | tf_op | source)
XLA Modules:
  0.0 45.3 jit_solution(14159977508703240987)
XLA Ops:
  0.6 42.0 %shard_map.68 = (f32[16,256]{1,0:T(8,128)}, f32[16,256]{1,0:T(8,128)}) custom-call(f32[16,256,256]{2,1,0:T(8,128)} %jac_hbm.1, f32[16,256]{1,0:T(8,128)} %obs_hbm.1, f32[1,256]{1,0:T(1,128)} %bitcast.2, f32[256,256]{1,0:T(8,128)} %smooth_hbm.1, f32[1,256]{1,0:T(1,128)} %bitcast.3), custom_call_target="tpu_custom_call" | custom-call | tf_op jit(solution)/shard_map/pallas_call | solution.py:404
  42.7 1.3 %copy.9 = f32[16,256]{1,0:T(8,128)} copy(f32[16,256]{1,0:T(8,128)} %get-tuple-element.4) | data formatting | bytes 32768
  44.0 1.3 %copy.10 = f32[16,256]{1,0:T(8,128)} copy(f32[16,256]{1,0:T(8,128)} %get-tuple-element.5) | data formatting | bytes 32768
